TPU v7x, 256 devices: a whole 4x4x8 slice. The times are simulated.
256 devices in a mesh: rep: 2 (over core), mp: 128 (over y, x, z).
Axes of the slice: x: 4, y: 4, z: 8, core: 2. Of those that a mesh axis runs over, the one named last changes fastest.
Arguments:
- lookup_block: int32 [2, 16384, 128, 4], P(None, ('rep', 'mp')), may hold values from 0 to 9
- lookup_offset: int32 [2, 16384, 128, 4], P(None, ('rep', 'mp')), may hold values from 0 to 63
- interaction_grad: bfloat16 [2, 16384, 128, 128], P(None, ('rep', 'mp')), may hold values from -1.25 to 1.25
- table: bfloat16 [393216, 256], P('mp'), may hold values from -0.3125 to 0.3125
- adagrad_state: float32 [393216], P('mp'), may hold values from 0.05 to 2
- touched_blocks: int32 [128, 10], P('mp'), may hold values from 0 to 47, as said below
- dither: int32 [128, 640, 256], P('mp'), may hold values from 0 to 32767
Outputs:
- new_table: bfloat16 [393216, 256], P('mp')
- new_state: float32 [393216], P('mp')
Inputs may be any that keep to these rules, and one draw needn't show every extreme that they name: `touched_blocks`: each row names 10 different row blocks.
All inputs are finite; a program needn't handle non-finite values.
Results may differ from a plain program's by a relative error of at most 0.00055.
The roundings to bfloat16 on the way count: a program that leaves them out, or rounds other values in their place, can miss the bound.
Values may be sent and summed in bfloat16 or wider, within the bound.
No kernel may reach another device: no remote copies, remote signals or barrier semaphores. Data moves between devices by JAX's collectives and lax.ppermute only.
A program may use at most 128 MiB of HBM per device.

v0:
```python
import jax
import jax.numpy as jnp
from jax import lax
from jax.sharding import PartitionSpec as P

BLOCK = 64


LEARN_RATE = 0.1
POOL_DECAY = 0.5
DITHER_UNIT = 2.0 ** (-15)
SMALLEST = 2.0 ** (-14)


def from_everyone(x, axis):
    peers = lax.axis_size(axis)
    return lax.all_to_all(jnp.broadcast_to(x[None], (peers, *x.shape)), axis, 0, 0, tiled=True)


def taken_together(x, axis):
    return from_everyone(x, axis).sum(axis=0)


def dither_round(weights, dither_bits):
    magnitude = jnp.maximum(jnp.abs(weights), SMALLEST)
    spacing = jnp.exp2(jnp.floor(jnp.log2(magnitude)) - 7.0)
    grid_level = jnp.floor(weights / spacing + dither_bits.astype(jnp.float32) * DITHER_UNIT)
    return (grid_level * spacing).astype(jnp.bfloat16)


def adagrad_rows(slab_rows, grad_rows, state_rows, dither_bits):
    state_next = state_rows + jnp.mean(grad_rows * grad_rows, axis=-1)
    moved = (
        slab_rows.astype(jnp.float32)
        - LEARN_RATE * grad_rows / (jnp.sqrt(state_next) + 1e-08)[:, None]
    )
    return (dither_round(moved, dither_bits), state_next)


def hit_counts(lookup_rows, slab_size):
    column = lax.broadcasted_iota(jnp.int32, (1, slab_size), 1)
    counted = jnp.zeros((lookup_rows.shape[0], slab_size), jnp.bfloat16)
    for lookup in range(lookup_rows.shape[1]):
        counted = counted + (lookup_rows[:, lookup : lookup + 1] == column).astype(jnp.bfloat16)
    return counted


def pairwise(pooled_rows, cotangent):
    forward = jnp.einsum("bfg,bge->bfe", cotangent, pooled_rows, preferred_element_type=jnp.float32)
    backward = jnp.einsum(
        "bgf,bge->bfe", cotangent, pooled_rows, preferred_element_type=jnp.float32
    )
    return (forward + backward + POOL_DECAY * pooled_rows.astype(jnp.float32)).astype(jnp.bfloat16)


def per_device(
    lookup_block, lookup_offset, interaction_grad, table, adagrad_state, touched_blocks, dither
):
    micro_count, sample_count, feature_count, bag_count = lookup_block.shape
    groups = lax.axis_size("mp")
    row_count, emb_width = table.shape
    touch_count = touched_blocks.shape[1]
    slab_size = touch_count * BLOCK
    owner_samples = groups * sample_count
    lookup_rows = lookup_block * BLOCK + lookup_offset
    owner_rows = lax.all_to_all(lookup_rows, "mp", split_axis=2, concat_axis=1, tiled=True)
    owner_rows = owner_rows.reshape(micro_count, owner_samples, bag_count)
    table_blocks = table.reshape(row_count // BLOCK, BLOCK, emb_width)
    slab_table = table_blocks[touched_blocks[0]].reshape(slab_size, emb_width)
    counted = [hit_counts(owner_rows[micro_index], slab_size) for micro_index in range(micro_count)]
    pooled_rows = [
        jnp.dot(hits, slab_table, preferred_element_type=jnp.float32).astype(jnp.bfloat16)
        for hits in counted
    ]
    returned = []
    for micro_index in range(micro_count):
        outgoing = pooled_rows[micro_index].reshape(groups, sample_count, 1, emb_width)
        arrived = lax.all_to_all(outgoing, "mp", split_axis=0, concat_axis=2, tiled=True)
        sample_pooled = arrived.reshape(sample_count, feature_count, emb_width)
        grad_rows = pairwise(sample_pooled, interaction_grad[micro_index])
        sent_back = lax.all_to_all(
            grad_rows.reshape(1, sample_count, feature_count, emb_width),
            "mp",
            split_axis=2,
            concat_axis=0,
            tiled=True,
        )
        returned.append(sent_back.reshape(owner_samples, emb_width))
    slab_grad = jnp.zeros((slab_size, emb_width), jnp.float32)
    for micro_index in range(micro_count):
        slab_grad = slab_grad + jnp.einsum(
            "sr,se->re",
            counted[micro_index],
            returned[micro_index],
            preferred_element_type=jnp.float32,
        )
    state_slab = adagrad_state.reshape(row_count // BLOCK, BLOCK)[touched_blocks[0]].reshape(
        slab_size
    )
    summed_grad = taken_together(slab_grad, "rep")
    new_rows, state_next = adagrad_rows(slab_table, summed_grad, state_slab, dither[0])
    updated_blocks = table_blocks.at[touched_blocks[0]].set(
        new_rows.reshape(touch_count, BLOCK, emb_width)
    )
    state_blocks = adagrad_state.reshape(row_count // BLOCK, BLOCK)
    updated_state = state_blocks.at[touched_blocks[0]].set(state_next.reshape(touch_count, BLOCK))
    return (updated_blocks.reshape(row_count, emb_width), updated_state.reshape(row_count))


def solution(mesh):
    return jax.shard_map(
        per_device,
        mesh=mesh,
        in_specs=(
            P(None, ("rep", "mp"), None, None),
            P(None, ("rep", "mp"), None, None),
            P(None, ("rep", "mp"), None, None),
            P("mp", None),
            P("mp"),
            P("mp", None),
            P("mp", None, None),
        ),
        out_specs=(P("mp", None), P("mp")),
        check_vma=False,
    )
```

profile of v0, /device:TPU:1, one launch (start us, length us, event | category | flops | bytes accessed | tf_op | source)
XLA Modules:
  0.0 486.4 jit_solution(15015553084337166868)
XLA Ops:
  0.6 1.4 copy.65
  2.0 1.1 copy_add_fusion
  3.1 0.3 copy.49
  3.4 1.2 reshape.158
  4.6 16.3 %all-to-all-start = ((s32[128,1,512]{2,1,0:T(1,128)}), s32[128,1,512]{2,1,0:T(1,128)S(1)}, u32[]{:S(2)}, u32[]{:S(2)}) async-start(s32[128,1,512]{2,1,0:T(1,128)} %reshape.158), calls=%async_computation | async-start | bytes 524288 | tf_op jit(solution)/shard_map/all_to_all | solution.py:66
  20.9 0.7 fusion.49
  21.6 0.6 gather_fusion
  22.2 12.3 %all-to-all-done = s32[128,1,512]{2,1,0:T(1,128)S(1)} async-done(((s32[128,1,512]{2,1,0:T(1,128)}), s32[128,1,512]{2,1,0:T(1,128)S(1)}, u32[]{:S(2)}, u32[]{:S(2)}) %all-to-all-start) | async-done | bytes 262176 | tf_op jit(solution)/shard_map/all_to_all | solution.py:66
  34.5 0.5 broadcast.66
  35.0 1.3 reduce
  36.2 0.3 reshape.159
  36.6 0.1 fusion.50
  36.7 0.1 squeeze.20
  36.8 0.1 fusion.52
  36.9 15.3 %convolution_convert_fusion.1 = bf16[8192,256]{1,0:T(8,128)(2,1)} fusion(bf16[640,256]{1,0:T(8,128)(2,1)S(1)} %bitcast.110, s32[8192]{0:T(1024)S(1)} %bitcast.114, s32[8192]{0:T(1024)S(1)} %bitcast.116, s32[8192]{0:T(1024)S(1)} %bitcast.118, s32[8192]{0:T(1024)S(1)} %bitcast.112), kind=kOutput, calls=%fused_computation.27 | convolution fusion | flops 2770337792 | bytes 4653056 | tf_op jit(solution)/shard_map/dot_general | solution.py:72
  52.2 7.4 %all-to-all-start.1 = ((bf16[128,64,1,256]{3,1,2,0:T(8,128)(2,1)}), bf16[128,64,1,256]{3,1,2,0:T(8,128)(2,1)}, u32[]{:S(2)}, u32[]{:S(2)}) async-start(bf16[128,64,1,256]{3,1,2,0:T(8,128)(2,1)} %bitcast.102), calls=%async_computation.1 | async-start | bytes 8388608 | tf_op jit(solution)/shard_map/all_to_all | solution.py:78
  59.6 0.1 squeeze.22
  59.8 0.1 fusion.51
  59.9 15.3 %convolution_convert_fusion = bf16[8192,256]{1,0:T(8,128)(2,1)} fusion(bf16[640,256]{1,0:T(8,128)(2,1)S(1)} %bitcast.111, s32[8192]{0:T(1024)S(1)} %bitcast.122, s32[8192]{0:T(1024)S(1)} %bitcast.124, s32[8192]{0:T(1024)S(1)} %bitcast.126, s32[8192]{0:T(1024)S(1)} %bitcast.120), kind=kOutput, calls=%fused_computation.26 | convolution fusion | flops 2770337792 | bytes 4653056 | tf_op jit(solution)/shard_map/dot_general | solution.py:72
  75.1 79.8 %all-to-all-done.1 = bf16[128,64,1,256]{3,1,2,0:T(8,128)(2,1)} async-done(((bf16[128,64,1,256]{3,1,2,0:T(8,128)(2,1)}), bf16[128,64,1,256]{3,1,2,0:T(8,128)(2,1)}, u32[]{:S(2)}, u32[]{:S(2)}) %all-to-all-start.1) | async-done | bytes 4194336 | tf_op jit(solution)/shard_map/all_to_all | solution.py:78
  154.9 7.9 %all-to-all-start.3 = ((bf16[128,64,1,256]{3,1,2,0:T(8,128)(2,1)}), bf16[128,64,1,256]{3,1,2,0:T(8,128)(2,1)}, u32[]{:S(2)}, u32[]{:S(2)}) async-start(bf16[128,64,1,256]{3,1,2,0:T(8,128)(2,1)} %bitcast.103), calls=%async_computation.3 | async-start | bytes 8388608 | tf_op jit(solution)/shard_map/all_to_all | solution.py:78
  162.8 6.9 %copy.52 = bf16[128,64,1,256]{0,3,1,2:T(8,128)(2,1)} copy(bf16[128,64,1,256]{3,1,2,0:T(8,128)(2,1)} %all-to-all-done.1) | data formatting | bytes 8388608 | tf_op jit(solution)/shard_map/all_to_all | solution.py:78
  169.7 4.2 fusion.28
  174.0 5.3 %fusion.22 = bf16[1,64,128,256]{2,3,1,0:T(8,128)(2,1)} fusion(f32[64,256,128]{2,1,0:T(8,128)S(1)} %fusion.28, bf16[128,64,1,256]{0,3,1,2:T(8,128)(2,1)S(1)} %copy-done, bf16[2,64,128,128]{3,2,1,0:T(8,128)(2,1)} %param.9), kind=kOutput, calls=%fused_computation.34 | convolution fusion | flops 547356672 | bytes 23068672 | tf_op jit(solution)/shard_map/bfg,bge->bfe/dot_general | solution.py:49
  179.3 6.8 %copy.53 = bf16[1,64,128,256]{3,1,0,2:T(8,128)(2,1)} copy(bf16[1,64,128,256]{2,3,1,0:T(8,128)(2,1)} %fusion.22) | data formatting | bytes 8388608 | tf_op jit(solution)/shard_map/reshape | solution.py:82
  186.1 69.3 %all-to-all-done.3 = bf16[128,64,1,256]{3,1,2,0:T(8,128)(2,1)} async-done(((bf16[128,64,1,256]{3,1,2,0:T(8,128)(2,1)}), bf16[128,64,1,256]{3,1,2,0:T(8,128)(2,1)}, u32[]{:S(2)}, u32[]{:S(2)}) %all-to-all-start.3) | async-done | bytes 4194336 | tf_op jit(solution)/shard_map/all_to_all | solution.py:78
  255.4 7.4 %all-to-all-start.2 = ((bf16[1,64,128,256]{3,1,0,2:T(8,128)(2,1)}), bf16[1,64,128,256]{3,1,0,2:T(8,128)(2,1)}, u32[]{:S(2)}, u32[]{:S(2)}) async-start(bf16[1,64,128,256]{3,1,0,2:T(8,128)(2,1)} %copy.53), calls=%async_computation.2 | async-start | bytes 8388608 | tf_op jit(solution)/shard_map/all_to_all | solution.py:81
  262.8 6.9 %copy.56 = bf16[128,64,1,256]{0,3,1,2:T(8,128)(2,1)} copy(bf16[128,64,1,256]{3,1,2,0:T(8,128)(2,1)} %all-to-all-done.3) | data formatting | bytes 8388608 | tf_op jit(solution)/shard_map/all_to_all | solution.py:78
  269.8 4.2 fusion.24
  274.0 5.3 %fusion.23 = bf16[1,64,128,256]{2,3,1,0:T(8,128)(2,1)} fusion(f32[64,256,128]{2,1,0:T(8,128)S(1)} %fusion.24, bf16[128,64,1,256]{0,3,1,2:T(8,128)(2,1)S(1)} %copy-done.1, bf16[2,64,128,128]{3,2,1,0:T(8,128)(2,1)} %param.9), kind=kOutput, calls=%fused_computation.35 | convolution fusion | flops 547356672 | bytes 23068672 | tf_op jit(solution)/shard_map/bfg,bge->bfe/dot_general | solution.py:49
  279.4 6.9 %copy.57 = bf16[1,64,128,256]{3,1,0,2:T(8,128)(2,1)} copy(bf16[1,64,128,256]{2,3,1,0:T(8,128)(2,1)} %fusion.23) | data formatting | bytes 8388608 | tf_op jit(solution)/shard_map/reshape | solution.py:82
  286.2 67.5 %all-to-all-done.2 = bf16[1,64,128,256]{3,1,0,2:T(8,128)(2,1)} async-done(((bf16[1,64,128,256]{3,1,0,2:T(8,128)(2,1)}), bf16[1,64,128,256]{3,1,0,2:T(8,128)(2,1)}, u32[]{:S(2)}, u32[]{:S(2)}) %all-to-all-start.2) | async-done | bytes 4194336 | tf_op jit(solution)/shard_map/all_to_all | solution.py:81
  353.7 7.6 %all-to-all-start.4 = ((bf16[1,64,128,256]{3,1,0,2:T(8,128)(2,1)}), bf16[1,64,128,256]{3,1,0,2:T(8,128)(2,1)}, u32[]{:S(2)}, u32[]{:S(2)}) async-start(bf16[1,64,128,256]{3,1,0,2:T(8,128)(2,1)} %copy.57), calls=%async_computation.4 | async-start | bytes 8388608 | tf_op jit(solution)/shard_map/all_to_all | solution.py:81
  361.3 0.1 reshape.121
  361.4 0.6 gather_fusion.1
  362.0 0.9 convert_multiply_fusion
  362.8 14.4 %fusion.14 = f32[640,256]{1,0:T(8,128)S(1)} fusion(bf16[8192,256]{1,0:T(8,128)(2,1)} %bitcast.22, s32[8192]{0:T(1024)S(1)} %bitcast.115, s32[8192]{0:T(1024)S(1)} %bitcast.117, s32[8192]{0:T(1024)S(1)} %bitcast.119, s32[8192]{0:T(1024)S(1)} %bitcast.113), kind=kOutput, calls=%fused_computation.28 | convolution fusion | flops 2768240640 | bytes 4980736 | tf_op jit(solution)/shard_map/sr,se->re/dot_general | solution.py:91
  377.2 72.3 %all-to-all-done.4 = bf16[1,64,128,256]{3,1,0,2:T(8,128)(2,1)} async-done(((bf16[1,64,128,256]{3,1,0,2:T(8,128)(2,1)}), bf16[1,64,128,256]{3,1,0,2:T(8,128)(2,1)}, u32[]{:S(2)}, u32[]{:S(2)}) %all-to-all-start.4) | async-done | bytes 4194336 | tf_op jit(solution)/shard_map/all_to_all | solution.py:81
  449.5 14.2 %fusion.44 = f32[640,256]{1,0:T(8,128)S(1)} fusion(f32[640,256]{1,0:T(8,128)S(1)} %fusion.14, bf16[8192,256]{1,0:T(8,128)(2,1)} %bitcast.40, s32[8192]{0:T(1024)S(1)} %bitcast.123, s32[8192]{0:T(1024)S(1)} %bitcast.125, s32[8192]{0:T(1024)S(1)} %bitcast.127, s32[8192]{0:T(1024)S(1)} %bitcast.121), kind=kOutput, calls=%fused_computation.52 | convolution fusion | flops 2768404480 | bytes 5636096 | tf_op jit(solution)/shard_map/sr,se->re/dot_general | solution.py:91
  463.7 0.1 broadcast_in_dim.2
  463.8 15.9 %all_to_all.80 = f32[2,640,256]{2,1,0:T(8,128)S(1)} all-to-all(f32[2,640,256]{2,1,0:T(8,128)S(1)} %broadcast_in_dim.2), channel_id=1, replica_groups=mesh['rep'=2,'mp'=128] {'rep'}, dimensions={0} | all-to-all | bytes 2621440 | tf_op jit(solution)/shard_map/all_to_all | solution.py:17
  479.7 0.1 reduce_sum.18
  479.8 0.2 multiply_reduce_fusion
  480.0 0.1 div.23
  480.1 1.9 scatter_custom_fusion.1
  482.0 1.7 multiply_convert_fusion
  483.7 1.0 scatter_fusion
  484.7 1.4 reshape.123
  (20 shorter events, 0.1 us)
Async XLA Ops:
  4.6 29.9 %all-to-all-start = ((s32[128,1,512]{2,1,0:T(1,128)}), s32[128,1,512]{2,1,0:T(1,128)S(1)}, u32[]{:S(2)}, u32[]{:S(2)}) async-start(s32[128,1,512]{2,1,0:T(1,128)} %reshape.158), calls=%async_computation | async-start | bytes 524288 | tf_op jit(solution)/shard_map/all_to_all | solution.py:66
  22.2 37.7 %copy-start.3 = (bf16[10,64,256]{2,1,0:T(8,128)(2,1)}, bf16[10,64,256]{2,1,0:T(8,128)(2,1)S(1)}, u32[]{:S(2)}) copy-start(bf16[10,64,256]{2,1,0:T(8,128)(2,1)S(1)} %gather_fusion) | copy-start | bytes 983044
  52.2 102.7 %all-to-all-start.1 = ((bf16[128,64,1,256]{3,1,2,0:T(8,128)(2,1)}), bf16[128,64,1,256]{3,1,2,0:T(8,128)(2,1)}, u32[]{:S(2)}, u32[]{:S(2)}) async-start(bf16[128,64,1,256]{3,1,2,0:T(8,128)(2,1)} %bitcast.102), calls=%async_computation.1 | async-start | bytes 8388608 | tf_op jit(solution)/shard_map/all_to_all | solution.py:78
  154.9 100.5 %all-to-all-start.3 = ((bf16[128,64,1,256]{3,1,2,0:T(8,128)(2,1)}), bf16[128,64,1,256]{3,1,2,0:T(8,128)(2,1)}, u32[]{:S(2)}, u32[]{:S(2)}) async-start(bf16[128,64,1,256]{3,1,2,0:T(8,128)(2,1)} %bitcast.103), calls=%async_computation.3 | async-start | bytes 8388608 | tf_op jit(solution)/shard_map/all_to_all | solution.py:78
  169.7 4.2 copy-start
  255.4 98.3 %all-to-all-start.2 = ((bf16[1,64,128,256]{3,1,0,2:T(8,128)(2,1)}), bf16[1,64,128,256]{3,1,0,2:T(8,128)(2,1)}, u32[]{:S(2)}, u32[]{:S(2)}) async-start(bf16[1,64,128,256]{3,1,0,2:T(8,128)(2,1)} %copy.53), calls=%async_computation.2 | async-start | bytes 8388608 | tf_op jit(solution)/shard_map/all_to_all | solution.py:81
  269.8 4.2 copy-start.1
  279.4 81.9 %copy-start.6 = (f32[3072]{0:T(1024)S(1)}, f32[3072]{0:T(1024)}, u32[]{:S(2)}) copy-start(f32[3072]{0:T(1024)} %param.11) | copy-start | bytes 36868
  279.4 82.6 %copy-start.4 = (s32[1,640,256]{2,1,0:T(8,128)S(1)}, s32[1,640,256]{2,1,0:T(8,128)}, u32[]{:S(2)}) copy-start(s32[1,640,256]{2,1,0:T(8,128)} %param.13) | copy-start | bytes 1966084
  353.7 95.8 %all-to-all-start.4 = ((bf16[1,64,128,256]{3,1,0,2:T(8,128)(2,1)}), bf16[1,64,128,256]{3,1,0,2:T(8,128)(2,1)}, u32[]{:S(2)}, u32[]{:S(2)}) async-start(bf16[1,64,128,256]{3,1,0,2:T(8,128)(2,1)} %copy.57), calls=%async_computation.4 | async-start | bytes 8388608 | tf_op jit(solution)/shard_map/all_to_all | solution.py:81
  361.4 15.8 %copy-start.5 = (f32[48,64]{1,0:T(8,128)}, f32[48,64]{1,0:T(8,128)S(1)}, u32[]{:S(2)}) copy-start(f32[48,64]{1,0:T(8,128)S(1)} %reshape.121) | copy-start | bytes 36868
  484.7 1.4 copy-start.2
where the time goes:
time: 495 us; the launch traced here: 486 us
  waiting for transfers between devices  301 us (61%)
  matrix products  78.3 us (16%)
  starting transfers between devices  46.5 us (9%)
  local copies, waits for them, and re-layouts  35.6 us (7%)
  blocking collectives  15.9 us (3%)
  other arithmetic  7.82 us (2%)
    all_to_all x2, waiting for transfers between devices, per_device(): lax.all_to_all(outgoing, 'mp', split_axis=0, concat_axis=2, tiled=True)  149 us
    all_to_all x2, waiting for transfers between devices, per_device(): lax.all_to_all(grad_rows.reshape(1, sample_count, feature_count, emb_widt...  140 us
    dot_general x2, matrix products, per_device(): jnp.dot(hits, slab_table, preferred_element_type=jnp.float32)  30.6 us
    dot_general x2, matrix products, per_device(): jnp.einsum('sr,se->re', counted[micro_index], returned[micro_index], pref...  28.5 us
    all_to_all x1, starting transfers between devices, per_device(): lax.all_to_all(lookup_rows, 'mp', split_axis=2, concat_axis=1, tiled=True)  16.3 us
    all_to_all x1, blocking collectives, from_everyone(): lax.all_to_all(jnp.broadcast_to(x[None], (peers, *x.shape)), axis, 0, 0,...  15.9 us
    all_to_all x2, starting transfers between devices, per_device(): lax.all_to_all(outgoing, 'mp', split_axis=0, concat_axis=2, tiled=True)  15.2 us
    all_to_all x2, starting transfers between devices, per_device(): lax.all_to_all(grad_rows.reshape(1, sample_count, feature_count, emb_widt...  14.9 us
  transfers between devices with their start and end apart: 5, of which 5 were waited for; matrix products, arithmetic and copies ran while one was open for 16% of the time, Pallas kernels for 0%

commit v1 on v0

v1 whole, which is shorter than its diff:
```python
import jax
import jax.numpy as jnp
from jax import lax
from jax.experimental import pallas as pl
from jax.experimental.pallas import tpu as pltpu
from jax.sharding import Mesh
from jax.sharding import PartitionSpec as P

BLOCK = 64
LEARN_RATE = 0.1
POOL_DECAY = 0.5
DITHER_UNIT = 2.0 ** (-15)
SMALLEST = 2.0 ** (-14)

NY, NX, NZ = 4, 4, 8
LINE = 4
HALF = 128
SLAB = 640
BAG = 4
AXES = ("rep", "y", "x", "z")


def device_id(r, y, x, z):
    return ((r * NY + y) * NX + x) * NZ + z


def line_groups():
    first = [[device_id(0, y, x, z) for x in range(NX)] for y in range(NY) for z in range(NZ)]
    second = [[device_id(1, y, x, z) for y in range(NY)] for x in range(NX) for z in range(NZ)]
    return first + second


def ring_pairs(step):
    pairs = []
    for y in range(NY):
        for x in range(NX):
            for z in range(NZ):
                pairs.append((device_id(0, y, x, z), device_id(0, (y + step) % NY, x, z)))
                pairs.append((device_id(1, y, x, z), device_id(1, y, (x + step) % NX, z)))
    return pairs


def ring_send(value, step):
    return lax.ppermute(value, AXES, ring_pairs(step))


def line_exchange(value):
    return lax.all_to_all(value, AXES, 0, 0, tiled=True, axis_index_groups=line_groups())


def swap_cores(value):
    return lax.ppermute(value, "rep", [(0, 1), (1, 0)])


def counts_of(columns, iota):
    one = jnp.ones((), jnp.bfloat16)
    zero = jnp.zeros((), jnp.bfloat16)
    total = None
    for column in columns:
        hit = jnp.where(column == iota, one, zero)
        total = hit if total is None else total + hit
    return total


def pool_kernel(k, chips, samples, idx_ref, slab_ref, *rest):
    out_ref, buffer = rest[-2:]
    rows = chips * samples
    idx = idx_ref[...].reshape(rows, 128)
    iota = lax.broadcasted_iota(jnp.int16, (rows, SLAB), 1)
    for z in range(NZ):
        base = k * 32 + z * BAG
        hits = counts_of([idx[:, base + j : base + j + 1] for j in range(BAG)], iota)
        rows_sum = jnp.dot(hits, slab_ref[z], preferred_element_type=jnp.float32)
        buffer[pl.ds(z, rows, stride=NZ), :] = rows_sum
    out_ref[...] = buffer[...].astype(jnp.bfloat16).reshape(chips, samples, 1, NZ, HALF)


def pool_rows(k, idx, slabs, previous):
    samples = idx.shape[1]
    chips = 2
    operands = [idx, slabs]
    in_specs = [
        pl.BlockSpec((chips, samples, 128), lambda i: (i, 0, 0)),
        pl.BlockSpec((NZ, SLAB, HALF), lambda i: (0, 0, 0)),
    ]
    aliases = {}
    if previous is not None:
        operands.append(previous)
        in_specs.append(pl.BlockSpec(memory_space=pl.ANY))
        aliases = {2: 0}
    return pl.pallas_call(
        lambda *refs: pool_kernel(k, chips, samples, *refs),
        out_shape=jax.ShapeDtypeStruct((LINE, samples, 4, NZ, HALF), jnp.bfloat16),
        grid=(LINE // chips,),
        in_specs=in_specs,
        out_specs=pl.BlockSpec((chips, samples, 1, NZ, HALF), lambda i: (i, 0, k, 0, 0)),
        scratch_shapes=[pltpu.VMEM((chips * samples * NZ, HALF), jnp.float32)],
        input_output_aliases=aliases,
        compiler_params=pltpu.CompilerParams(vmem_limit_bytes=48 << 20),
        cost_estimate=pl.CostEstimate(
            flops=2 * LINE * samples * NZ * SLAB * 256, transcendentals=0, bytes_accessed=3 << 20
        ),
        name=f"pool_{k}",
    )(*operands)


def pair_kernel(place_ref, cot_ref, pooled_ref, out_ref):
    core = place_ref[0]
    ring = place_ref[1]
    samples = cot_ref.shape[0]

    def spots():
        for a in range(4):
            for b in range(4):
                line_at = jnp.where(core == 0, b, a)
                ring_at = jnp.where(core == 0, a, b)
                yield line_at, (ring_at - ring + 4) & 3

    spot_list = list(spots())
    for s in range(samples):
        pieces = [pooled_ref[line_at, s, k].astype(jnp.float32) for line_at, k in spot_list]
        wide = jnp.concatenate(pieces, axis=0)
        narrow = wide.astype(jnp.bfloat16)
        cot = cot_ref[s]
        total = jnp.dot(cot, narrow, preferred_element_type=jnp.float32)
        total = total + lax.dot_general(
            cot, narrow, (((0,), (0,)), ((), ())), preferred_element_type=jnp.float32
        )
        total = total + POOL_DECAY * wide
        for at, (line_at, k) in enumerate(spot_list):
            out_ref[line_at, s, k] = total[at * NZ : (at + 1) * NZ].astype(jnp.bfloat16)


def pair_rows(place, cotangent, pooled):
    samples = cotangent.shape[0]
    step = 8
    return pl.pallas_call(
        pair_kernel,
        out_shape=jax.ShapeDtypeStruct(pooled.shape, jnp.bfloat16),
        grid_spec=pltpu.PrefetchScalarGridSpec(
            num_scalar_prefetch=1,
            grid=(samples // step,),
            in_specs=[
                pl.BlockSpec((step, 128, 128), lambda i, place: (i, 0, 0)),
                pl.BlockSpec((LINE, step, 4, NZ, HALF), lambda i, place: (0, i, 0, 0, 0)),
            ],
            out_specs=pl.BlockSpec((LINE, step, 4, NZ, HALF), lambda i, place: (0, i, 0, 0, 0)),
        ),
        compiler_params=pltpu.CompilerParams(vmem_limit_bytes=48 << 20),
        cost_estimate=pl.CostEstimate(
            flops=4 * samples * 128 * 128 * 256, transcendentals=0, bytes_accessed=12 << 20
        ),
        name="pairwise",
    )(place, cotangent, pooled)


def spread_kernel(idx_low, idx_high, grads_ref, *rest):
    added = len(rest) == 5
    before_low, before_high = rest[:2] if added else (None, None)
    out_low, out_high, buffer = rest[-3:]
    rows = buffer.shape[0] // NZ
    step = pl.program_id(0)

    @pl.when(step == 0)
    def _():
        buffer[...] = grads_ref[...].reshape(rows * NZ, HALF).astype(jnp.float32)

    iota = lax.broadcasted_iota(jnp.int16, (SLAB, rows), 0)
    for idx_ref, before, out, shift in (
        (idx_low, before_low, out_low, 0),
        (idx_high, before_high, out_high, NZ // 2),
    ):
        grads = buffer[pl.ds(step + shift, rows, stride=NZ), :].astype(jnp.bfloat16)
        hits = counts_of([idx_ref[0, j : j + 1, :] for j in range(BAG)], iota)
        total = jnp.dot(hits, grads, preferred_element_type=jnp.float32)
        if added:
            total = total + before[0]
        out[0] = total


def spread_rows(k, idx, grads, previous):
    samples = grads.shape[1]
    rows = LINE * samples
    half = NZ // 2
    operands = [idx, idx, grads]
    in_specs = [
        pl.BlockSpec((1, BAG, rows), lambda i: (k * NZ + i, 0, 0)),
        pl.BlockSpec((1, BAG, rows), lambda i: (k * NZ + half + i, 0, 0)),
        pl.BlockSpec((LINE, samples, 1, NZ, HALF), lambda i: (0, 0, k, 0, 0)),
    ]
    out_spec = pl.BlockSpec((1, SLAB, HALF), lambda i: (i, 0, 0))
    aliases = {}
    if previous is not None:
        operands += list(previous)
        in_specs += [out_spec, out_spec]
        aliases = {3: 0, 4: 1}
    shape = jax.ShapeDtypeStruct((half, SLAB, HALF), jnp.float32)
    return pl.pallas_call(
        spread_kernel,
        out_shape=(shape, shape),
        grid=(half,),
        in_specs=in_specs,
        out_specs=(out_spec, out_spec),
        scratch_shapes=[pltpu.VMEM((rows * NZ, HALF), jnp.float32)],
        input_output_aliases=aliases,
        compiler_params=pltpu.CompilerParams(vmem_limit_bytes=48 << 20),
        cost_estimate=pl.CostEstimate(
            flops=2 * rows * NZ * SLAB * 256, transcendentals=0, bytes_accessed=6 << 20
        ),
        name=f"spread_{k}",
    )(*operands)


def dither_round(weights, dither_bits):
    magnitude = jnp.maximum(jnp.abs(weights), SMALLEST)
    spacing = jnp.exp2(jnp.floor(jnp.log2(magnitude)) - 7.0)
    grid_level = jnp.floor(weights / spacing + dither_bits.astype(jnp.float32) * DITHER_UNIT)
    return (grid_level * spacing).astype(jnp.bfloat16)


def adagrad_rows(slab_rows, grad_rows, state_rows, dither_bits):
    state_next = state_rows + jnp.mean(grad_rows * grad_rows, axis=-1)
    moved = (
        slab_rows.astype(jnp.float32)
        - LEARN_RATE * grad_rows / (jnp.sqrt(state_next) + 1e-08)[:, None]
    )
    return (dither_round(moved, dither_bits), state_next)


def per_device(
    lookup_block, lookup_offset, interaction_grad, table, adagrad_state, touched_blocks, dither
):
    core = lax.axis_index("rep")
    y = lax.axis_index("y")
    x = lax.axis_index("x")
    ring = jnp.where(core == 0, y, x)
    place = jnp.stack([core, ring]).astype(jnp.int32)
    row_count, emb_width = table.shape
    micro_count, sample_count = lookup_block.shape[:2]
    samples = micro_count * sample_count
    touch_count = touched_blocks.shape[1]

    table_blocks = table.reshape(row_count // BLOCK, BLOCK, emb_width)
    slab_table = table_blocks[touched_blocks[0]].reshape(SLAB, emb_width)
    own_half = lax.dynamic_slice(slab_table, (0, core * HALF), (SLAB, HALF))
    own_slabs = lax.all_gather(own_half, "z", axis=0, tiled=False)

    def flat(v):
        return v.transpose(0, 1, 3, 2).reshape(samples, 512).astype(jnp.bfloat16)

    own_lookups = jnp.concatenate([flat(lookup_block), flat(lookup_offset)], axis=1)
    both = jnp.concatenate([own_lookups, swap_cores(own_lookups)], axis=0)
    other_cot = swap_cores(interaction_grad)
    lane = lax.broadcasted_iota(jnp.int32, (512, 1), 0)
    bag_at = lane // 128
    y_at, x_at, z_at = (lane // 32) % 4, (lane // 8) % 4, lane % 8
    line_at = jnp.where(core == 0, x_at, y_at)
    ring_at = (jnp.where(core == 0, y_at, x_at) - ring + 4) % 4
    goes_to = line_at * 128 + ring_at * 32 + z_at * BAG + bag_at
    moves = goes_to == lax.broadcasted_iota(jnp.int32, (512, 512), 1)
    moves = jnp.concatenate([jnp.where(moves, 64.0, 0.0), jnp.where(moves, 1.0, 0.0)], axis=0)
    rows_out = jnp.dot(both, moves.astype(jnp.bfloat16), preferred_element_type=jnp.float32)
    rows_out = rows_out.reshape(2 * samples, LINE, 128).transpose(1, 0, 2)
    rows_in = line_exchange(rows_out).astype(jnp.int16)
    by_sample = [rows_in[:, c * samples : (c + 1) * samples] for c in range(2)]
    by_lookup = [
        v.astype(jnp.int32).reshape(LINE * samples, 128).T.astype(jnp.int16).reshape(
            32, BAG, LINE * samples
        )
        for v in by_sample
    ]

    from_left = ring_send(own_slabs, 1)
    from_right = ring_send(own_slabs, -1)
    across = jnp.concatenate(
        [ring_send(from_left[:4], 1), ring_send(from_right[4:], -1)], axis=0
    )
    slabs = {0: own_slabs, 1: from_right, 2: across, 3: from_left}

    cots = [
        interaction_grad.reshape(samples, 128, 128),
        other_cot.reshape(samples, 128, 128),
    ]
    pooled = [None, None]
    for k in (0, 3, 1, 2):
        for c in range(2):
            pooled[c] = pool_rows(k, by_sample[c], slabs[k], pooled[c])
    grads = []
    for c in range(2):
        arrived = line_exchange(pooled[c])
        grads.append(line_exchange(pair_rows(place, cots[c], arrived)))
    partial = {}
    for k in (2, 1, 3, 0):
        partial[k] = spread_rows(k, by_lookup[0], grads[0], None)
    for k in (2, 1, 3, 0):
        partial[k] = spread_rows(k, by_lookup[1], grads[1], partial[k])

    low_one = ring_send(partial[1][0] + ring_send(partial[2][0], 1), 1)
    high_three = ring_send(partial[3][1] + ring_send(partial[2][1], -1), -1)
    high_one = ring_send(partial[1][1], 1)
    low_three = ring_send(partial[3][0], -1)
    on_ring = jnp.concatenate(
        [partial[0][0] + low_one + low_three, partial[0][1] + high_one + high_three], axis=0
    )
    own_grad = lax.psum_scatter(on_ring, "z", scatter_dimension=0, tiled=True)[0]
    other_grad = swap_cores(own_grad)
    summed_grad = jnp.where(
        core == 0,
        jnp.concatenate([own_grad, other_grad], axis=1),
        jnp.concatenate([other_grad, own_grad], axis=1),
    )

    state_blocks = adagrad_state.reshape(row_count // BLOCK, BLOCK)
    state_slab = state_blocks[touched_blocks[0]].reshape(SLAB)
    new_rows, state_next = adagrad_rows(slab_table, summed_grad, state_slab, dither[0])
    updated_blocks = table_blocks.at[touched_blocks[0]].set(
        new_rows.reshape(touch_count, BLOCK, emb_width)
    )
    updated_state = state_blocks.at[touched_blocks[0]].set(state_next.reshape(touch_count, BLOCK))
    return (updated_blocks.reshape(row_count, emb_width), updated_state.reshape(row_count))


def solution(mesh):
    fine = Mesh(mesh.devices.reshape(2, NY, NX, NZ), AXES)
    tables = ("y", "x", "z")
    return jax.shard_map(
        per_device,
        mesh=fine,
        in_specs=(
            P(None, AXES, None, None),
            P(None, AXES, None, None),
            P(None, AXES, None, None),
            P(tables, None),
            P(tables),
            P(tables, None),
            P(tables, None, None),
        ),
        out_specs=(P(tables, None), P(tables)),
        check_vma=False,
    )
```

time: 495 us -> 354 us (0.72)
  waiting for transfers between devices: 301 us -> 158 us
  Pallas kernels: 0 us -> 95.9 us
  matrix products: 78.3 us -> 2.36 us
  blocking collectives: 15.9 us -> 0 us
  between operations: 1.11 us -> 14.8 us
  local copies, waits for them, and re-layouts: 35.6 us -> 22.8 us
    all_to_all x5, waiting for transfers between devices: 301 us -> 54.6 us  [line_exchange(): lax.all_to_all(value, AXES, 0, 0, tiled=True, axis_index_groups=line_grou...]
    pallas_call x0 -> x18, Pallas kernels: none -> 95.9 us  [the longest x8 37.5 us: pool_rows(): pl.pallas_call(lambda *refs: pool_kernel(k, chips, samples, *refs), out_s...]
    dot_general x8 -> x1, matrix products: 78.3 us -> 2.36 us  [per_device(): jnp.dot(both, moves.astype(jnp.bfloat16), preferred_element_type=jnp.floa...]
    reduce_scatter x0 -> x1, waiting for transfers between devices: none -> 44.4 us  [per_device(): lax.psum_scatter(on_ring, 'z', scatter_dimension=0, tiled=True)[0]]
    all_gather x0 -> x1, waiting for transfers between devices: none -> 39.1 us  [per_device(): own_slabs = lax.all_gather(own_half, 'z', axis=0, tiled=False)]
    ppermute x0 -> x13, starting transfers between devices: none -> 26.3 us  [the longest x3 13.2 us: swap_cores(): return lax.ppermute(value, 'rep', [(0, 1), (1, 0)])]
    all_to_all x5, starting transfers between devices: 46.5 us -> 23.1 us  [line_exchange(): lax.all_to_all(value, AXES, 0, 0, tiled=True, axis_index_groups=line_grou...]
    ppermute x0 -> x13, waiting for transfers between devices: none -> 20.1 us  [the longest x10 18.1 us: ring_send(): return lax.ppermute(value, AXES, ring_pairs(step))]
  transfers between devices with their start and end apart: 5 -> 20, of which waited for: 5 -> 12; matrix products, arithmetic and copies ran while one was open for 16% -> 3% of each run, Pallas kernels for 0% -> 25%
where the time goes in v1:
time: 354 us; the launch traced here: 348 us
  waiting for transfers between devices  158 us (45%)
  Pallas kernels  95.9 us (27%)
  starting transfers between devices  49.7 us (14%)
  local copies, waits for them, and re-layouts  22.8 us (6%)
  between operations  14.8 us (4%)
  other arithmetic  4.2 us (1%)
    all_to_all x5, waiting for transfers between devices, line_exchange(): lax.all_to_all(value, AXES, 0, 0, tiled=True, axis_index_groups=line_grou...  54.6 us
    reduce_scatter x1, waiting for transfers between devices, per_device(): lax.psum_scatter(on_ring, 'z', scatter_dimension=0, tiled=True)[0]  44.4 us
    all_gather x1, waiting for transfers between devices, per_device(): own_slabs = lax.all_gather(own_half, 'z', axis=0, tiled=False)  39.1 us
    pallas_call x8, Pallas kernels, pool_rows(): pl.pallas_call(lambda *refs: pool_kernel(k, chips, samples, *refs), out_s...  37.5 us
    pallas_call x8, Pallas kernels, spread_rows(): pl.pallas_call(spread_kernel, out_shape=(shape, shape), grid=(half,), in_...  33.5 us
    pallas_call x2, Pallas kernels, pair_rows(): pl.pallas_call(pair_kernel, out_shape=jax.ShapeDtypeStruct(pooled.shape,...  25 us
    all_to_all x5, starting transfers between devices, line_exchange(): lax.all_to_all(value, AXES, 0, 0, tiled=True, axis_index_groups=line_grou...  23.1 us
    ppermute x10, waiting for transfers between devices, ring_send(): return lax.ppermute(value, AXES, ring_pairs(step))  18.1 us
  transfers between devices with their start and end apart: 20, of which 12 were waited for; matrix products, arithmetic and copies ran while one was open for 3% of the time, Pallas kernels for 25%

profile of v1, /device:TPU:1, one launch (start us, length us, event | category | flops | bytes accessed | tf_op | source)
XLA Modules:
  0.0 348.1 jit_solution(18346404360946891691)
XLA Ops:
  7.2 1.4 copy.53
  10.0 39.1 %all-gather.3.cloned.1.call-done = bf16[5120,128]{1,0:T(8,128)(2,1)} async-done(((bf16[640,128]{1,0:T(8,128)(2,1)}), bf16[5120,128]{1,0:T(8,128)(2,1)}) %all-gather.3.cloned.1.call-update) | async-done | bytes 1310736 | tf_op jit(solution)/shard_map/all_gather | solution.py:246
  50.4 1.6 collective-permute-start.4
  53.4 5.4 %collective-permute-start = (bf16[128,1024]{1,0:T(8,128)(2,1)}, bf16[128,1024]{1,0:T(8,128)(2,1)}, u32[]{:S(2)}, u32[]{:S(2)}) collective-permute-start(bf16[128,1024]{1,0:T(8,128)(2,1)} %bitcast_dynamic-update-slice_fusion), channel_id=1, source_target_pairs={{0,128},{128,0},{1,129},{129,1},{2,130},{130,2},{3,131},{131,3},{4... | collective-permute-start | bytes 786440 | tf_op jit(solution)/shard_map/ppermute | solution.py:52
  60.3 2.4 fusion
  62.6 2.0 copy.26
  64.7 3.5 all-to-all-start
  70.2 5.9 %all-to-all-done = f32[4,256,128]{2,1,0:T(8,128)S(1)} async-done(((f32[4,256,128]{2,1,0:T(8,128)}), f32[4,256,128]{2,1,0:T(8,128)S(1)}, u32[]{:S(2)}, u32[]{:S(2)}) %all-to-all-start) | async-done | bytes 524320 | tf_op jit(solution)/shard_map/all_to_all | solution.py:48
  76.2 3.0 collective-permute-start.5
  79.3 4.7 %pool_0.3.refs_2_ = bf16[4,128,4,8,128]{4,3,2,1,0:T(8,128)(2,1)S(1)} custom-call(s16[4,128,128]{2,1,0:T(8,128)(2,1)S(1)} %get-tuple-element.34.refs_0_, bf16[8,640,128]{2,1,0:T(8,128)(2,1)S(1)} %bitcast.34), custom_call_target="tpu_custom_call" | custom-call | flops 1342177280 | bytes 3145728 | tf_op jit(solution)/shard_map/pool_0/pallas_call | solution.py:91
  84.0 4.7 %pool_3.3.refs_2_ = bf16[4,128,4,8,128]{4,3,2,1,0:T(8,128)(2,1)S(1)} custom-call(s16[4,128,128]{2,1,0:T(8,128)(2,1)S(1)} %get-tuple-element.34.refs_0_, bf16[8,640,128]{2,1,0:T(8,128)(2,1)S(1)} %collective-permute-done.2.refs_1_, bf16[4,128,4,8,128]{4,3,2,1,0:T(8,128)(2,1)S(1)} %pool_0.3.refs_2_), custom_call_target="tpu_custom_call", output_to_operand_aliasing={{}: (2, {})} | custom-call | flops 1342177280 | bytes 3145728 | tf_op jit(solution)/shard_map/pool_3/pallas_call | solution.py:91
  88.7 4.7 %pool_1.3.refs_2_ = bf16[4,128,4,8,128]{4,3,2,1,0:T(8,128)(2,1)S(1)} custom-call(s16[4,128,128]{2,1,0:T(8,128)(2,1)S(1)} %get-tuple-element.34.refs_0_, bf16[8,640,128]{2,1,0:T(8,128)(2,1)S(1)} %collective-permute-done.4.refs_1_, bf16[4,128,4,8,128]{4,3,2,1,0:T(8,128)(2,1)S(1)} %pool_3.3.refs_2_), custom_call_target="tpu_custom_call", output_to_operand_aliasing={{}: (2, {})} | custom-call | flops 1342177280 | bytes 3145728 | tf_op jit(solution)/shard_map/pool_1/pallas_call | solution.py:91
  94.6 4.7 %pool_2.3 = bf16[4,128,4,8,128]{4,3,2,1,0:T(8,128)(2,1)S(1)} custom-call(s16[4,128,128]{2,1,0:T(8,128)(2,1)S(1)} %get-tuple-element.34.refs_0_, bf16[8,640,128]{2,1,0:T(8,128)(2,1)S(1)} %constant_dynamic-update-slice_fusion.refs_1_, bf16[4,128,4,8,128]{4,3,2,1,0:T(8,128)(2,1)S(1)} %pool_1.3.refs_2_), custom_call_target="tpu_custom_call", output_to_operand_aliasing={{}: (2, {})} | custom-call | flops 1342177280 | bytes 3145728 | tf_op jit(solution)/shard_map/pool_2/pallas_call | solution.py:91
  99.3 2.0 copy-done.1
  102.4 5.0 %all-to-all-start.3 = ((bf16[4,128,4,8,128]{4,3,2,1,0:T(8,128)(2,1)}), bf16[4,128,4,8,128]{4,3,2,1,0:T(8,128)(2,1)}, u32[]{:S(2)}, u32[]{:S(2)}) async-start(bf16[4,128,4,8,128]{4,3,2,1,0:T(8,128)(2,1)} %copy-done.1), calls=%async_computation.3 | async-start | bytes 8388608 | tf_op jit(solution)/shard_map/all_to_all | solution.py:48
  107.5 1.3 copy-done.7
  108.8 4.7 %pool_0.2.refs_2_ = bf16[4,128,4,8,128]{4,3,2,1,0:T(8,128)(2,1)S(1)} custom-call(s16[4,128,128]{2,1,0:T(8,128)(2,1)S(1)} %get-tuple-element.35.refs_0_, bf16[8,640,128]{2,1,0:T(8,128)(2,1)S(1)} %bitcast.35), custom_call_target="tpu_custom_call" | custom-call | flops 1342177280 | bytes 3145728 | tf_op jit(solution)/shard_map/pool_0/pallas_call | solution.py:91
  113.5 4.7 %pool_3.2.refs_2_ = bf16[4,128,4,8,128]{4,3,2,1,0:T(8,128)(2,1)S(1)} custom-call(s16[4,128,128]{2,1,0:T(8,128)(2,1)S(1)} %get-tuple-element.35.refs_0_, bf16[8,640,128]{2,1,0:T(8,128)(2,1)S(1)} %collective-permute-done.2.refs_1_, bf16[4,128,4,8,128]{4,3,2,1,0:T(8,128)(2,1)S(1)} %pool_0.2.refs_2_), custom_call_target="tpu_custom_call", output_to_operand_aliasing={{}: (2, {})} | custom-call | flops 1342177280 | bytes 3145728 | tf_op jit(solution)/shard_map/pool_3/pallas_call | solution.py:91
  118.2 4.7 %pool_1.2.refs_2_ = bf16[4,128,4,8,128]{4,3,2,1,0:T(8,128)(2,1)S(1)} custom-call(s16[4,128,128]{2,1,0:T(8,128)(2,1)S(1)} %get-tuple-element.35.refs_0_, bf16[8,640,128]{2,1,0:T(8,128)(2,1)S(1)} %collective-permute-done.4.refs_1_, bf16[4,128,4,8,128]{4,3,2,1,0:T(8,128)(2,1)S(1)} %pool_3.2.refs_2_), custom_call_target="tpu_custom_call", output_to_operand_aliasing={{}: (2, {})} | custom-call | flops 1342177280 | bytes 3145728 | tf_op jit(solution)/shard_map/pool_1/pallas_call | solution.py:91
  122.9 4.7 %pool_2.2 = bf16[4,128,4,8,128]{4,3,2,1,0:T(8,128)(2,1)S(1)} custom-call(s16[4,128,128]{2,1,0:T(8,128)(2,1)S(1)} %get-tuple-element.35.refs_0_, bf16[8,640,128]{2,1,0:T(8,128)(2,1)S(1)} %copy-done.5, bf16[4,128,4,8,128]{4,3,2,1,0:T(8,128)(2,1)S(1)} %pool_1.2.refs_2_), custom_call_target="tpu_custom_call", output_to_operand_aliasing={{}: (2, {})} | custom-call | flops 1342177280 | bytes 3145728 | tf_op jit(solution)/shard_map/pool_2/pallas_call | solution.py:91
  127.6 1.9 copy-done
  129.5 4.9 %all-to-all-done.3.pooled_ref = bf16[4,128,4,8,128]{4,3,2,1,0:T(8,128)(2,1)} async-done(((bf16[4,128,4,8,128]{4,3,2,1,0:T(8,128)(2,1)}), bf16[4,128,4,8,128]{4,3,2,1,0:T(8,128)(2,1)}, u32[]{:S(2)}, u32[]{:S(2)}) %all-to-all-start.3) | async-done | bytes 4194336 | tf_op jit(solution)/shard_map/all_to_all | solution.py:48
  134.4 4.9 %all-to-all-start.1 = ((bf16[4,128,4,8,128]{4,3,2,1,0:T(8,128)(2,1)}), bf16[4,128,4,8,128]{4,3,2,1,0:T(8,128)(2,1)}, u32[]{:S(2)}, u32[]{:S(2)}) async-start(bf16[4,128,4,8,128]{4,3,2,1,0:T(8,128)(2,1)} %copy-done), calls=%async_computation.1 | async-start | bytes 8388608 | tf_op jit(solution)/shard_map/all_to_all | solution.py:48
  139.3 3.1 collective-permute-start.1
  142.5 12.5 %pairwise.3 = bf16[4,128,4,8,128]{4,3,2,1,0:T(8,128)(2,1)S(1)} custom-call(s32[2]{0:T(128)S(1)} %pad_add_fusion.place_ref, bf16[128,128,128]{2,1,0:T(8,128)(2,1)} %bitcast.38, bf16[4,128,4,8,128]{4,3,2,1,0:T(8,128)(2,1)} %all-to-all-done.3.pooled_ref), custom_call_target="tpu_custom_call" | custom-call | flops 2147483648 | bytes 12582912 | tf_op jit(solution)/shard_map/pairwise/pallas_call | solution.py:137
  155.0 2.0 copy-done.3
  156.9 9.3 %all-to-all-done.1.pooled_ref = bf16[4,128,4,8,128]{4,3,2,1,0:T(8,128)(2,1)} async-done(((bf16[4,128,4,8,128]{4,3,2,1,0:T(8,128)(2,1)}), bf16[4,128,4,8,128]{4,3,2,1,0:T(8,128)(2,1)}, u32[]{:S(2)}, u32[]{:S(2)}) %all-to-all-start.1) | async-done | bytes 4194336 | tf_op jit(solution)/shard_map/all_to_all | solution.py:48
  166.2 4.9 %all-to-all-start.4 = ((bf16[4,128,4,8,128]{4,3,2,1,0:T(8,128)(2,1)}), bf16[4,128,4,8,128]{4,3,2,1,0:T(8,128)(2,1)}, u32[]{:S(2)}, u32[]{:S(2)}) async-start(bf16[4,128,4,8,128]{4,3,2,1,0:T(8,128)(2,1)} %copy-done.3), calls=%async_computation.4 | async-start | bytes 8388608 | tf_op jit(solution)/shard_map/all_to_all | solution.py:48
  171.1 12.5 %pairwise.2 = bf16[4,128,4,8,128]{4,3,2,1,0:T(8,128)(2,1)S(1)} custom-call(s32[2]{0:T(128)S(1)} %pad_add_fusion.place_ref, bf16[128,128,128]{2,1,0:T(8,128)(2,1)} %bitcast.11.cot_ref, bf16[4,128,4,8,128]{4,3,2,1,0:T(8,128)(2,1)} %all-to-all-done.1.pooled_ref), custom_call_target="tpu_custom_call" | custom-call | flops 2147483648 | bytes 12582912 | tf_op jit(solution)/shard_map/pairwise/pallas_call | solution.py:137
  183.6 2.0 copy-done.2
  185.6 12.4 %all-to-all-done.4.grads_ref = bf16[4,128,4,8,128]{4,3,2,1,0:T(8,128)(2,1)} async-done(((bf16[4,128,4,8,128]{4,3,2,1,0:T(8,128)(2,1)}), bf16[4,128,4,8,128]{4,3,2,1,0:T(8,128)(2,1)}, u32[]{:S(2)}, u32[]{:S(2)}) %all-to-all-start.4) | async-done | bytes 4194336 | tf_op jit(solution)/shard_map/all_to_all | solution.py:48
  198.0 4.9 %all-to-all-start.2 = ((bf16[4,128,4,8,128]{4,3,2,1,0:T(8,128)(2,1)}), bf16[4,128,4,8,128]{4,3,2,1,0:T(8,128)(2,1)}, u32[]{:S(2)}, u32[]{:S(2)}) async-start(bf16[4,128,4,8,128]{4,3,2,1,0:T(8,128)(2,1)} %copy-done.2), calls=%async_computation.2 | async-start | bytes 8388608 | tf_op jit(solution)/shard_map/all_to_all | solution.py:48
  203.6 4.1 %spread_2.2 = (f32[4,640,128]{2,1,0:T(8,128)S(1)}, f32[4,640,128]{2,1,0:T(8,128)S(1)}) custom-call(s16[32,4,512]{2,1,0:T(4,128)(2,1)S(1)} %reshape.290.idx_low.idx_high, s16[32,4,512]{2,1,0:T(4,128)(2,1)S(1)} %reshape.290.idx_low.idx_high, bf16[4,128,4,8,128]{4,3,2,1,0:T(8,128)(2,1)} %all-to-all-done.4.grads_ref), custom_call_target="tpu_custom_call" | custom-call | flops 1342177280 | bytes 6291456 | tf_op jit(solution)/shard_map/spread_2/pallas_call | solution.py:198
  207.7 22.1 %all-to-all-done.2.grads_ref = bf16[4,128,4,8,128]{4,3,2,1,0:T(8,128)(2,1)} async-done(((bf16[4,128,4,8,128]{4,3,2,1,0:T(8,128)(2,1)}), bf16[4,128,4,8,128]{4,3,2,1,0:T(8,128)(2,1)}, u32[]{:S(2)}, u32[]{:S(2)}) %all-to-all-start.2) | async-done | bytes 4194336 | tf_op jit(solution)/shard_map/all_to_all | solution.py:48
  229.9 4.3 %spread_2.3 = (f32[4,640,128]{2,1,0:T(8,128)S(1)}, f32[4,640,128]{2,1,0:T(8,128)S(1)}) custom-call(s16[32,4,512]{2,1,0:T(4,128)(2,1)S(1)} %reshape.287.idx_low.idx_high, s16[32,4,512]{2,1,0:T(4,128)(2,1)S(1)} %reshape.287.idx_low.idx_high, bf16[4,128,4,8,128]{4,3,2,1,0:T(8,128)(2,1)} %all-to-all-done.2.grads_ref, ...), custom_call_target="tpu_custom_call", output_to_operand_aliasing={{0}: (3, {}), {1}: (4, {})} | custom-call | flops 1342177280 | bytes 6291456 | tf_op jit(solution)/shard_map/spread_2/pallas_call | solution.py:198
  235.7 4.1 %spread_1.2 = (f32[4,640,128]{2,1,0:T(8,128)S(1)}, f32[4,640,128]{2,1,0:T(8,128)S(1)}) custom-call(s16[32,4,512]{2,1,0:T(4,128)(2,1)S(1)} %reshape.290.idx_low.idx_high, s16[32,4,512]{2,1,0:T(4,128)(2,1)S(1)} %reshape.290.idx_low.idx_high, bf16[4,128,4,8,128]{4,3,2,1,0:T(8,128)(2,1)} %all-to-all-done.4.grads_ref), custom_call_target="tpu_custom_call" | custom-call | flops 1342177280 | bytes 6291456 | tf_op jit(solution)/shard_map/spread_1/pallas_call | solution.py:198
  239.8 4.3 %spread_1.3 = (f32[4,640,128]{2,1,0:T(8,128)S(1)}, f32[4,640,128]{2,1,0:T(8,128)S(1)}) custom-call(s16[32,4,512]{2,1,0:T(4,128)(2,1)S(1)} %reshape.287.idx_low.idx_high, s16[32,4,512]{2,1,0:T(4,128)(2,1)S(1)} %reshape.287.idx_low.idx_high, bf16[4,128,4,8,128]{4,3,2,1,0:T(8,128)(2,1)} %all-to-all-done.2.grads_ref, ...), custom_call_target="tpu_custom_call", output_to_operand_aliasing={{0}: (3, {}), {1}: (4, {})} | custom-call | flops 1342177280 | bytes 6291456 | tf_op jit(solution)/shard_map/spread_1/pallas_call | solution.py:198
  244.1 4.1 %spread_3.2 = (f32[4,640,128]{2,1,0:T(8,128)S(1)}, f32[4,640,128]{2,1,0:T(8,128)S(1)}) custom-call(s16[32,4,512]{2,1,0:T(4,128)(2,1)S(1)} %reshape.290.idx_low.idx_high, s16[32,4,512]{2,1,0:T(4,128)(2,1)S(1)} %reshape.290.idx_low.idx_high, bf16[4,128,4,8,128]{4,3,2,1,0:T(8,128)(2,1)} %all-to-all-done.4.grads_ref), custom_call_target="tpu_custom_call" | custom-call | flops 1342177280 | bytes 6291456 | tf_op jit(solution)/shard_map/spread_3/pallas_call | solution.py:198
  248.2 4.3 %spread_3.3 = (f32[4,640,128]{2,1,0:T(8,128)S(1)}, f32[4,640,128]{2,1,0:T(8,128)S(1)}) custom-call(s16[32,4,512]{2,1,0:T(4,128)(2,1)S(1)} %reshape.287.idx_low.idx_high, s16[32,4,512]{2,1,0:T(4,128)(2,1)S(1)} %reshape.287.idx_low.idx_high, bf16[4,128,4,8,128]{4,3,2,1,0:T(8,128)(2,1)} %all-to-all-done.2.grads_ref, ...), custom_call_target="tpu_custom_call", output_to_operand_aliasing={{0}: (3, {}), {1}: (4, {})} | custom-call | flops 1342177280 | bytes 6291456 | tf_op jit(solution)/shard_map/spread_3/pallas_call | solution.py:198
  252.7 2.7 collective-permute-start.11
  257.3 4.1 %spread_0.2 = (f32[4,640,128]{2,1,0:T(8,128)S(1)}, f32[4,640,128]{2,1,0:T(8,128)S(1)}) custom-call(s16[32,4,512]{2,1,0:T(4,128)(2,1)S(1)} %reshape.290.idx_low.idx_high, s16[32,4,512]{2,1,0:T(4,128)(2,1)S(1)} %reshape.290.idx_low.idx_high, bf16[4,128,4,8,128]{4,3,2,1,0:T(8,128)(2,1)} %all-to-all-done.4.grads_ref), custom_call_target="tpu_custom_call" | custom-call | flops 1342177280 | bytes 6291456 | tf_op jit(solution)/shard_map/spread_0/pallas_call | solution.py:198
  261.4 4.3 %spread_0.3 = (f32[4,640,128]{2,1,0:T(8,128)S(1)}, f32[4,640,128]{2,1,0:T(8,128)S(1)}) custom-call(s16[32,4,512]{2,1,0:T(4,128)(2,1)S(1)} %reshape.287.idx_low.idx_high, s16[32,4,512]{2,1,0:T(4,128)(2,1)S(1)} %reshape.287.idx_low.idx_high, bf16[4,128,4,8,128]{4,3,2,1,0:T(8,128)(2,1)} %all-to-all-done.2.grads_ref, ...), custom_call_target="tpu_custom_call", output_to_operand_aliasing={{0}: (3, {}), {1}: (4, {})} | custom-call | flops 1342177280 | bytes 6291456 | tf_op jit(solution)/shard_map/spread_0/pallas_call | solution.py:198
  266.8 3.2 collective-permute-done.11
  270.1 13.9 %collective-permute-done.8 = f32[4,640,128]{2,1,0:T(8,128)S(1)} collective-permute-done((f32[4,640,128]{2,1,0:T(8,128)S(1)}, f32[4,640,128]{2,1,0:T(8,128)S(1)}, u32[]{:S(2)}, u32[]{:S(2)}) %collective-permute-start.8) | collective-permute-done | bytes 1310752 | tf_op jit(solution)/shard_map/ppermute | solution.py:44
  284.2 1.6 pad_maximum_fusion
  285.9 44.4 %reduce-scatter.2.cloned.1.call-done = f32[1,640,128]{2,1,0:T(8,128)} async-done(((f32[8,640,128]{2,1,0:T(8,128)}), f32[1,640,128]{2,1,0:T(8,128)}) %reduce-scatter.2.cloned.1.call-update) | async-done | bytes 327696 | tf_op jit(solution)/shard_map/reduce_scatter | solution.py:305
  330.3 4.7 %collective-permute-start.12 = (f32[640,128]{1,0:T(8,128)}, f32[640,128]{1,0:T(8,128)S(1)}, u32[]{:S(2)}, u32[]{:S(2)}) collective-permute-start(f32[640,128]{1,0:T(8,128)} %bitcast.45), channel_id=1, source_target_pairs={{0,128},{128,0},{1,129},{129,1},{2,130},{130,2},{3,131},{131,3},{4... | collective-permute-start | bytes 983048 | tf_op jit(solution)/shard_map/ppermute | solution.py:52
  337.9 2.4 scatter_fusion
  (82 shorter events, 19.5 us)
Async XLA Ops:
  7.2 1.5 copy-start.14
  7.2 41.9 %all-gather.3.cloned.1.call-start = ((), (), s32[]{:S(2)}) async-start(), calls=%async_computation.7 | async-start | bytes 1474560 | tf_op jit(solution)/shard_map/all_gather | solution.py:246
  8.6 40.5 %copy-start.8 = (bf16[3072,256]{1,0:T(8,128)(2,1)}, bf16[3072,256]{1,0:T(8,128)(2,1)S(1)}, u32[]{:S(2)}) copy-start(bf16[3072,256]{1,0:T(8,128)(2,1)S(1)} %copy.53) | copy-start | bytes 4718596
  8.6 41.7 %copy-start.11 = (s32[2,64,128,4]{2,3,1,0:T(4,128)S(1)}, s32[2,64,128,4]{2,3,1,0:T(4,128)}, u32[]{:S(2)}) copy-start(s32[2,64,128,4]{2,3,1,0:T(4,128)} %param.7) | copy-start | bytes 786436
  8.6 41.7 %copy-start.12 = (s32[2,64,128,4]{2,3,1,0:T(4,128)S(1)}, s32[2,64,128,4]{2,3,1,0:T(4,128)}, u32[]{:S(2)}) copy-start(s32[2,64,128,4]{2,3,1,0:T(4,128)} %param.8) | copy-start | bytes 786436
  49.1 19.0 %collective-permute-start.2 = (bf16[8,640,128]{2,1,0:T(8,128)(2,1)}, bf16[8,640,128]{2,1,0:T(8,128)(2,1)S(1)}, u32[]{:S(2)}, u32[]{:S(2)}) collective-permute-start(bf16[8,640,128]{2,1,0:T(8,128)(2,1)} %bitcast.32), channel_id=1, source_target_pairs={{0,32},{128,136},{1,33},{129,137},{2,34},{130,138},{3,35},{131,139... | collective-permute-start | bytes 3932168 | tf_op jit(solution)/shard_map/ppermute | solution.py:44
  50.4 25.7 %collective-permute-start.4 = (bf16[8,640,128]{2,1,0:T(8,128)(2,1)}, bf16[8,640,128]{2,1,0:T(8,128)(2,1)S(1)}, u32[]{:S(2)}, u32[]{:S(2)}) collective-permute-start(bf16[8,640,128]{2,1,0:T(8,128)(2,1)} %bitcast.33), channel_id=1, source_target_pairs={{0,96},{128,152},{1,97},{129,153},{2,98},{130,154},{3,99},{131,155... | collective-permute-start | bytes 3932168 | tf_op jit(solution)/shard_map/ppermute | solution.py:44
  53.4 6.9 %collective-permute-start = (bf16[128,1024]{1,0:T(8,128)(2,1)}, bf16[128,1024]{1,0:T(8,128)(2,1)}, u32[]{:S(2)}, u32[]{:S(2)}) collective-permute-start(bf16[128,1024]{1,0:T(8,128)(2,1)} %bitcast_dynamic-update-slice_fusion), channel_id=1, source_target_pairs={{0,128},{128,0},{1,129},{129,1},{2,130},{130,2},{3,131},{131,3},{4... | collective-permute-start | bytes 786440 | tf_op jit(solution)/shard_map/ppermute | solution.py:52
  64.7 11.4 %all-to-all-start = ((f32[4,256,128]{2,1,0:T(8,128)}), f32[4,256,128]{2,1,0:T(8,128)S(1)}, u32[]{:S(2)}, u32[]{:S(2)}) async-start(f32[4,256,128]{2,1,0:T(8,128)} %bitcast.43), calls=%async_computation | async-start | bytes 1048576 | tf_op jit(solution)/shard_map/all_to_all | solution.py:48
  69.0 24.4 %collective-permute-start.3 = (bf16[4,640,128]{2,1,0:T(8,128)(2,1)}, bf16[4,640,128]{2,1,0:T(8,128)(2,1)}, u32[]{:S(2)}, u32[]{:S(2)}) collective-permute-start(bf16[4,640,128]{2,1,0:T(8,128)(2,1)} %slice.21), channel_id=1, source_target_pairs={{0,32},{128,136},{1,33},{129,137},{2,34},{130,138},{3,35},{131,139... | collective-permute-start | bytes 1966088 | tf_op jit(solution)/shard_map/ppermute | solution.py:44
  76.1 3.2 copy-start.6
  76.2 18.3 %collective-permute-start.5 = (bf16[4,640,128]{2,1,0:T(8,128)(2,1)S(1)}, bf16[4,640,128]{2,1,0:T(8,128)(2,1)S(1)}, u32[]{:S(2)}, u32[]{:S(2)}) collective-permute-start(bf16[4,640,128]{2,1,0:T(8,128)(2,1)S(1)} %slice.22), channel_id=1, source_target_pairs={{0,96},{128,152},{1,97},{129,153},{2,98},{130,154},{3,99},{131,155... | collective-permute-start | bytes 1966088 | tf_op jit(solution)/shard_map/ppermute | solution.py:44
  99.3 2.0 copy-start.1
  101.4 1.1 copy-start.4
  102.4 32.0 %all-to-all-start.3 = ((bf16[4,128,4,8,128]{4,3,2,1,0:T(8,128)(2,1)}), bf16[4,128,4,8,128]{4,3,2,1,0:T(8,128)(2,1)}, u32[]{:S(2)}, u32[]{:S(2)}) async-start(bf16[4,128,4,8,128]{4,3,2,1,0:T(8,128)(2,1)} %copy-done.1), calls=%async_computation.3 | async-start | bytes 8388608 | tf_op jit(solution)/shard_map/all_to_all | solution.py:48
  107.5 1.3 copy-start.7
  118.2 4.7 %copy-start.5 = (bf16[8,640,128]{2,1,0:T(8,128)(2,1)S(1)}, bf16[8,640,128]{2,1,0:T(8,128)(2,1)}, u32[]{:S(2)}) copy-start(bf16[8,640,128]{2,1,0:T(8,128)(2,1)} %copy-done.4) | copy-start | bytes 3932164
  127.6 1.9 copy-start
  134.4 31.8 %all-to-all-start.1 = ((bf16[4,128,4,8,128]{4,3,2,1,0:T(8,128)(2,1)}), bf16[4,128,4,8,128]{4,3,2,1,0:T(8,128)(2,1)}, u32[]{:S(2)}, u32[]{:S(2)}) async-start(bf16[4,128,4,8,128]{4,3,2,1,0:T(8,128)(2,1)} %copy-done), calls=%async_computation.1 | async-start | bytes 8388608 | tf_op jit(solution)/shard_map/all_to_all | solution.py:48
  139.3 31.8 %collective-permute-start.1 = (bf16[2,64,128,128]{3,2,1,0:T(8,128)(2,1)}, bf16[2,64,128,128]{3,2,1,0:T(8,128)(2,1)}, u32[]{:S(2)}, u32[]{:S(2)}) collective-permute-start(bf16[2,64,128,128]{3,2,1,0:T(8,128)(2,1)} %param.9), channel_id=1, source_target_pairs={{0,128},{128,0},{1,129},{129,1},{2,130},{130,2},{3,131},{131,3},{4... | collective-permute-start | bytes 12582920 | tf_op jit(solution)/shard_map/ppermute | solution.py:52
  155.0 2.0 copy-start.3
  166.2 31.8 %all-to-all-start.4 = ((bf16[4,128,4,8,128]{4,3,2,1,0:T(8,128)(2,1)}), bf16[4,128,4,8,128]{4,3,2,1,0:T(8,128)(2,1)}, u32[]{:S(2)}, u32[]{:S(2)}) async-start(bf16[4,128,4,8,128]{4,3,2,1,0:T(8,128)(2,1)} %copy-done.3), calls=%async_computation.4 | async-start | bytes 8388608 | tf_op jit(solution)/shard_map/all_to_all | solution.py:48
  183.6 2.0 copy-start.2
  198.0 31.8 %all-to-all-start.2 = ((bf16[4,128,4,8,128]{4,3,2,1,0:T(8,128)(2,1)}), bf16[4,128,4,8,128]{4,3,2,1,0:T(8,128)(2,1)}, u32[]{:S(2)}, u32[]{:S(2)}) async-start(bf16[4,128,4,8,128]{4,3,2,1,0:T(8,128)(2,1)} %copy-done.2), calls=%async_computation.2 | async-start | bytes 8388608 | tf_op jit(solution)/shard_map/all_to_all | solution.py:48
  202.9 127.4 %reduce-scatter.2.cloned.1.call-start = ((), (), s32[]{:S(2)}) async-start(), calls=%async_computation.6 | async-start | bytes 2949120 | tf_op jit(solution)/shard_map/reduce_scatter | solution.py:305
  234.1 18.4 %collective-permute-start.10 = (f32[4,640,128]{2,1,0:T(8,128)S(1)}, f32[4,640,128]{2,1,0:T(8,128)S(1)}, u32[]{:S(2)}, u32[]{:S(2)}) collective-permute-start(f32[4,640,128]{2,1,0:T(8,128)S(1)} %get-tuple-element.33), channel_id=1, source_target_pairs={{0,96},{128,152},{1,97},{129,153},{2,98},{130,154},{3,99},{131,155... | collective-permute-start | bytes 3932168 | tf_op jit(solution)/shard_map/ppermute | solution.py:44
  234.8 21.2 %collective-permute-start.6 = (f32[4,640,128]{2,1,0:T(8,128)S(1)}, f32[4,640,128]{2,1,0:T(8,128)S(1)}, u32[]{:S(2)}, u32[]{:S(2)}) collective-permute-start(f32[4,640,128]{2,1,0:T(8,128)S(1)} %get-tuple-element.26), channel_id=1, source_target_pairs={{0,32},{128,136},{1,33},{129,137},{2,34},{130,138},{3,35},{131,139... | collective-permute-start | bytes 3932168 | tf_op jit(solution)/shard_map/ppermute | solution.py:44
  244.0 22.7 %collective-permute-start.9 = (f32[4,640,128]{2,1,0:T(8,128)S(1)}, f32[4,640,128]{2,1,0:T(8,128)S(1)}, u32[]{:S(2)}, u32[]{:S(2)}) collective-permute-start(f32[4,640,128]{2,1,0:T(8,128)S(1)} %get-tuple-element.31), channel_id=1, source_target_pairs={{0,32},{128,136},{1,33},{129,137},{2,34},{130,138},{3,35},{131,139... | collective-permute-start | bytes 3932168 | tf_op jit(solution)/shard_map/ppermute | solution.py:44
  252.7 17.3 %collective-permute-start.11 = (f32[4,640,128]{2,1,0:T(8,128)S(1)}, f32[4,640,128]{2,1,0:T(8,128)S(1)}, u32[]{:S(2)}, u32[]{:S(2)}) collective-permute-start(f32[4,640,128]{2,1,0:T(8,128)S(1)} %add.166), channel_id=1, source_target_pairs={{0,96},{128,152},{1,97},{129,153},{2,98},{130,154},{3,99},{131,155... | collective-permute-start | bytes 3932168 | tf_op jit(solution)/shard_map/ppermute | solution.py:44
  255.4 28.6 %collective-permute-start.8 = (f32[4,640,128]{2,1,0:T(8,128)S(1)}, f32[4,640,128]{2,1,0:T(8,128)S(1)}, u32[]{:S(2)}, u32[]{:S(2)}) collective-permute-start(f32[4,640,128]{2,1,0:T(8,128)S(1)} %get-tuple-element.29), channel_id=1, source_target_pairs={{0,96},{128,152},{1,97},{129,153},{2,98},{130,154},{3,99},{131,155... | collective-permute-start | bytes 3932168 | tf_op jit(solution)/shard_map/ppermute | solution.py:44
  256.1 27.9 %collective-permute-start.7 = (f32[4,640,128]{2,1,0:T(8,128)S(1)}, f32[4,640,128]{2,1,0:T(8,128)S(1)}, u32[]{:S(2)}, u32[]{:S(2)}) collective-permute-start(f32[4,640,128]{2,1,0:T(8,128)S(1)} %add.162), channel_id=1, source_target_pairs={{0,32},{128,136},{1,33},{129,137},{2,34},{130,138},{3,35},{131,139... | collective-permute-start | bytes 3932168 | tf_op jit(solution)/shard_map/ppermute | solution.py:44
  285.8 49.1 %copy-start.13 = (f32[3072]{0:T(1024)S(1)}, f32[3072]{0:T(1024)}, u32[]{:S(2)}) copy-start(f32[3072]{0:T(1024)} %param.11) | copy-start | bytes 36868
  285.8 49.8 %copy-start.10 = (s32[1,640,256]{2,1,0:T(8,128)S(1)}, s32[1,640,256]{2,1,0:T(8,128)}, u32[]{:S(2)}) copy-start(s32[1,640,256]{2,1,0:T(8,128)} %param.13) | copy-start | bytes 1966084
  330.3 6.1 %copy-start.9 = (f32[1,640,128]{2,1,0:T(8,128)S(1)}, f32[1,640,128]{2,1,0:T(8,128)}, u32[]{:S(2)}) copy-start(f32[1,640,128]{2,1,0:T(8,128)} %reduce-scatter.2.cloned.1.call-done) | copy-start | bytes 983044
  330.3 6.1 %collective-permute-start.12 = (f32[640,128]{1,0:T(8,128)}, f32[640,128]{1,0:T(8,128)S(1)}, u32[]{:S(2)}, u32[]{:S(2)}) collective-permute-start(f32[640,128]{1,0:T(8,128)} %bitcast.45), channel_id=1, source_target_pairs={{0,128},{128,0},{1,129},{129,1},{2,130},{130,2},{3,131},{131,3},{4... | collective-permute-start | bytes 983048 | tf_op jit(solution)/shard_map/ppermute | solution.py:52
Sparse Core Ops, SparseCore 0:
  10.1 38.9 all-gather.2
  286.0 44.2 reduce-scatter.1
